TPU v7x, 32 devices: a whole 2x2x4 slice. The times are simulated.
32 devices in a mesh: wide: 16 (over z, y, core), shard: 2 (over x).
Axes of the slice: x: 2, y: 2, z: 4, core: 2. Of those that a mesh axis runs over, the one named last changes fastest.
Arguments:
- weights: bfloat16 [256, 8192], P('shard'), may hold values from -6 to 6
- momentum: bfloat16 [16, 256, 8192], P('wide', 'shard'), may hold values from -6 to 6
- grads: bfloat16 [2, 16, 256, 8192], P(None, 'wide', 'shard'), may hold values from -6 to 6
- offsets: int32 [2, 64], P('shard'), may hold values from 0 to 96
- owners: int32 [2, 64], P('shard'), may hold values from 0 to 63, each once within a row
- exp_avg: float32 [2, 64, 32, 128], P('shard', 'wide'), may hold values from -7 to 7
- exp_sq: float32 [2, 64, 32, 128], P('shard', 'wide'), may hold values from 0.01 to 1
Outputs:
- new_weights: bfloat16 [256, 8192], P('shard')
- new_momentum: bfloat16 [16, 256, 8192], P('wide', 'shard')
- new_avg: float32 [2, 64, 32, 128], P('shard', 'wide')
- new_sq: float32 [2, 64, 32, 128], P('shard', 'wide')
- scales: float32 [2], replicated
Inputs may be any that keep to these rules, and one draw needn't show every extreme that they name: `offsets`: each block's band spans 32 consecutive transform rows. Each row of owners is a permutation of 0 to 63.
All inputs are finite; a program needn't handle non-finite values.
Results may differ from a plain program's by a relative error of at most 0.003.
Values may be sent and summed in bfloat16 or wider, within the bound.
No kernel may reach another device: no remote copies, remote signals or barrier semaphores. Data moves between devices by JAX's collectives and lax.ppermute only.
A program may use at most 128 MiB of HBM per device.

v0:
```python
import jax
import jax.numpy as jnp
from jax import lax
from jax.sharding import PartitionSpec as P

STEPS = 2
highest = lax.Precision.HIGHEST
momentum_decay = 0.9
beta_one = 0.8
beta_two = 0.95
adam_eps = 1e-08
rms_eps = 1e-06
learning_rate = 0.2


def dct_table(length):
    frequency = jnp.arange(length, dtype=jnp.float32)[:, None]
    position = jnp.arange(length, dtype=jnp.float32)[None, :]
    cosines = jnp.cos(jnp.pi * (2.0 * position + 1.0) * frequency / (2.0 * length))
    scaling = jnp.where(frequency == 0.0, jnp.sqrt(1.0 / length), jnp.sqrt(2.0 / length))
    return cosines * scaling


def band_tables(basis, offsets, band_rows):
    indices = offsets[:, :, None] + jnp.arange(band_rows, dtype=jnp.int32)[None, None, :]
    return basis[indices]


def inverse(coefs, picked, basis):
    right_part = jnp.einsum("rjpc,cb->rjpb", coefs, basis, precision=highest)
    return jnp.einsum("rjpa,rjpb->rajb", picked, right_part, precision=highest)


def per_device(weights, momentum, grads, offsets, owners, exp_avg, exp_sq):
    block_len = exp_avg.shape[3]
    band_rows = exp_avg.shape[2]
    basis = dct_table(block_len)
    picked = band_tables(basis, offsets, band_rows)
    slot_order = jnp.argsort(owners, axis=1)
    row_blocks = offsets.shape[0]
    col_blocks = offsets.shape[1]
    block_shape = (row_blocks, block_len, col_blocks, block_len)
    replicas = lax.axis_size("wide")
    count_all = exp_avg.size * lax.axis_size("wide") * lax.axis_size("shard")
    weight_now = weights.astype(jnp.float32).reshape(block_shape)
    moment_now = momentum[0].astype(jnp.float32).reshape(block_shape)
    avg_now = exp_avg
    sq_now = exp_sq
    scales = []
    for step_index in range(STEPS):
        blended = momentum_decay * moment_now + grads[step_index, 0].astype(jnp.float32).reshape(
            block_shape
        )
        left_part = jnp.einsum("rjpa,rajb->rjpb", picked, blended, precision=highest)
        band_coef = jnp.einsum("rjpb,cb->rjpc", left_part, basis, precision=highest)
        moment_now = blended - inverse(band_coef, picked, basis)
        slot_band = jnp.take_along_axis(band_coef, slot_order[:, :, None, None], axis=1)
        pieces = lax.all_to_all(
            slot_band.astype(jnp.bfloat16), "wide", split_axis=1, concat_axis=0, tiled=True
        ).astype(slot_band.dtype)
        summed = jnp.sum(pieces.reshape((replicas, row_blocks) + pieces.shape[1:]), axis=0)
        mean_band = summed / replicas
        avg_now = beta_one * avg_now + (1.0 - beta_one) * mean_band
        sq_now = beta_two * sq_now + (1.0 - beta_two) * mean_band * mean_band
        raw_update = avg_now / (jnp.sqrt(sq_now) + adam_eps)
        power_sum = lax.psum(jnp.sum(raw_update * raw_update), ("wide", "shard"))
        spread = jnp.sqrt(power_sum / count_all + rms_eps)
        update = (raw_update / spread).astype(jnp.bfloat16)
        gathered = lax.all_gather(update, "wide", axis=1, tiled=True)
        block_update = jnp.take_along_axis(
            gathered.astype(jnp.float32), owners[:, :, None, None], axis=1
        )
        weight_now = weight_now - learning_rate * inverse(block_update, picked, basis)
        scales.append(spread)
    new_weights = weight_now.reshape(weights.shape).astype(jnp.bfloat16)
    new_momentum = moment_now.reshape(momentum.shape).astype(jnp.bfloat16)
    return (new_weights, new_momentum, avg_now, sq_now, jnp.stack(scales))


def solution(mesh):
    in_specs = (
        P("shard", None),
        P("wide", "shard", None),
        P(None, "wide", "shard", None),
        P("shard", None),
        P("shard", None),
        P("shard", "wide", None, None),
        P("shard", "wide", None, None),
    )
    out_specs = (
        P("shard", None),
        P("wide", "shard", None),
        P("shard", "wide", None, None),
        P("shard", "wide", None, None),
        P(),
    )
    return jax.shard_map(
        per_device, mesh=mesh, in_specs=in_specs, out_specs=out_specs, check_vma=False
    )
```

profile of v0, /device:TPU:0, one launch (start us, length us, event | category | flops | bytes accessed | tf_op | source)
XLA Modules:
  0.0 231.6 jit_solution(10638912373604838056)
XLA Ops:
  3.4 6.6 %slice_convert_fusion.1 = (f32[1,1,128,8192]{3,2,1,0:T(8,128)}, f32[16,8,64,128]{3,1,2,0:T(8,128)S(1)}, f32[1,1,128,8192]{3,2,1,0:T(8,128)}) fusion(bf16[2,1,128,8192]{3,2,1,0:T(8,128)(2,1)} %param.11), kind=kLoop, calls=%fused_computation.20 | loop fusion | flops 2097152 | bytes 16777216 | tf_op jit(solution)/shard_map/convert_element_type | solution.py:51
  10.0 2.7 %copy.56 = f32[16,8,64,128]{3,2,1,0:T(8,128)} copy(f32[16,8,64,128]{3,1,2,0:T(8,128)S(1)} %get-tuple-element.34) | data formatting | bytes 8388608
  12.7 2.5 %convert_multiply_fusion = (f32[1,128,8192]{2,1,0:T(8,128)}, f32[16,8,64,128]{3,1,2,0:T(8,128)S(1)}) fusion(bf16[1,128,8192]{2,1,0:T(8,128)(2,1)S(1)} %copy-done.2), kind=kLoop, calls=%fused_computation.18 | loop fusion | flops 2097152 | bytes 10485760 | tf_op jit(solution)/shard_map/mul | solution.py:51
  15.3 2.7 %copy.55 = f32[16,8,64,128]{3,2,1,0:T(8,128)} copy(f32[16,8,64,128]{3,1,2,0:T(8,128)S(1)} %get-tuple-element.37) | data formatting | bytes 8388608
  18.2 6.0 %gather_fusion = f32[2048,128]{1,0:T(8,128)S(1)} fusion(f32[128,128]{1,0:T(8,128)S(1)} %cosine_multiply_fusion, s32[2048]{0:T(1024)S(1)} %broadcast_clamp_fusion), kind=kCustom, calls=%fused_computation.4 | custom fusion | bytes 2105344 | tf_op jit(solution)/shard_map/gather | solution.py:26
  24.2 12.7 %fusion.6 = f32[64,32,128]{2,1,0:T(8,128)S(1)} fusion(f32[64,32,128]{2,1,0:T(8,128)S(1)} %bitcast.197, f32[128,64,128]{2,1,0:T(8,128)} %bitcast.204, f32[128,64,128]{2,1,0:T(8,128)} %bitcast.205), kind=kOutput, calls=%fused_computation.16 | convolution fusion | flops 403701760 | bytes 10485760 | tf_op jit(solution)/shard_map/rjpa,rajb->rjpb/dot_general | solution.py:54
  39.3 5.6 %copy.44 = f32[1,1,128,8192]{2,3,1,0:T(8,128)} copy(f32[1,1,128,8192]{3,2,1,0:T(8,128)} %get-tuple-element.33) | data formatting | bytes 8388608 | tf_op jit(solution)/shard_map/convert_element_type | solution.py:51
  44.9 5.6 %copy.45 = f32[1,1,128,8192]{2,3,1,0:T(8,128)} copy(f32[1,1,128,8192]{3,2,1,0:T(8,128)} %get-tuple-element.35) | data formatting | bytes 8388608 | tf_op jit(solution)/shard_map/convert_element_type | solution.py:51
  50.5 5.6 %copy.43 = f32[1,128,8192]{1,2,0:T(8,128)} copy(f32[1,128,8192]{2,1,0:T(8,128)} %get-tuple-element.36) | data formatting | bytes 8388608 | tf_op jit(solution)/shard_map/mul | solution.py:51
  56.1 10.1 %fusion.3 = f32[1,128,64,128]{1,3,2,0:T(8,128)S(1)} fusion(f32[1,128,64,128]{1,3,2,0:T(8,128)} %bitcast.207, f32[1,128,64,128]{1,3,2,0:T(8,128)} %bitcast.208, f32[1,128,64,128]{1,3,2,0:T(8,128)} %bitcast.206, f32[64,32,128]{2,1,0:T(8,128)S(1)} %fusion.27, f32[64,32,128]{2,1,0:T(8,128)S(1)} %bitcast.198), kind=kOutput, calls=%fused_computation.11 | convolution fusion | flops 406847488 | bytes 18874368 | tf_op jit(solution)/shard_map/rjpa,rjpb->rajb/dot_general | solution.py:31
  66.2 6.7 %fusion.4 = f32[64,32,128]{2,1,0:T(8,128)S(1)} fusion(f32[64,32,128]{2,1,0:T(8,128)S(1)} %bitcast.199, f32[1,128,64,128]{1,3,2,0:T(8,128)S(1)} %fusion.3), kind=kOutput, calls=%fused_computation.13 | convolution fusion | flops 402653184 | bytes 6291456 | tf_op jit(solution)/shard_map/rjpa,rajb->rjpb/dot_general | solution.py:54
  78.5 7.4 %all-to-all-start.1 = ((bf16[1,64,32,128]{3,2,0,1:T(8,128)(2,1)}), bf16[1,64,32,128]{3,2,0,1:T(8,128)(2,1)S(1)}, u32[]{:S(2)}, u32[]{:S(2)}) async-start(bf16[1,64,32,128]{3,2,0,1:T(8,128)(2,1)} %get-tuple-element.39), calls=%async_computation.1 | async-start | bytes 1048576 | tf_op jit(solution)/shard_map/all_to_all | solution.py:58
  88.1 12.1 %all-to-all-done.1 = bf16[1,64,32,128]{3,2,0,1:T(8,128)(2,1)S(1)} async-done(((bf16[1,64,32,128]{3,2,0,1:T(8,128)(2,1)}), bf16[1,64,32,128]{3,2,0,1:T(8,128)(2,1)S(1)}, u32[]{:S(2)}, u32[]{:S(2)}) %all-to-all-start.1) | async-done | bytes 524320 | tf_op jit(solution)/shard_map/all_to_all | solution.py:58
  101.0 4.5 %all-to-all-start = ((bf16[1,64,32,128]{3,2,0,1:T(8,128)(2,1)}), bf16[1,64,32,128]{3,2,0,1:T(8,128)(2,1)}, u32[]{:S(2)}, u32[]{:S(2)}) async-start(bf16[1,64,32,128]{3,2,0,1:T(8,128)(2,1)} %get-tuple-element.40), calls=%async_computation | async-start | bytes 1048576 | tf_op jit(solution)/shard_map/all_to_all | solution.py:58
  105.5 8.7 %fusion = bf16[1,128,64,128]{1,3,2,0:T(8,128)(2,1)S(1)} fusion(f32[1,128,64,128]{1,3,2,0:T(8,128)} %copy-done, f32[64,32,128]{2,1,0:T(8,128)} %fusion.22, f32[64,32,128]{2,1,0:T(8,128)S(1)} %bitcast.200), kind=kOutput, calls=%fused_computation.6 | convolution fusion | flops 404750336 | bytes 8388608 | tf_op jit(solution)/shard_map/rjpa,rjpb->rajb/dot_general | solution.py:31
  114.1 2.9 %copy.51 = bf16[1,128,8192]{2,1,0:T(8,128)(2,1)} copy(bf16[1,128,8192]{1,2,0:T(8,128)(2,1)S(1)} %bitcast.210) | data formatting | bytes 4194304
  117.0 4.4 %copy.35 = f32[128,8192]{0,1:T(8,128)} copy(bf16[128,8192]{1,0:T(8,128)(2,1)} %param.9) | data formatting | bytes 6291456 | tf_op jit(solution)/shard_map/reshape | solution.py:45
  123.4 40.9 %all-reduce = (f32[]{:T(128)}, f32[]{:T(128)}) all-reduce(f32[]{:T(128)} %get-tuple-element.38, f32[]{:T(128)} %get-tuple-element.30), channel_id=1, replica_groups=mesh['wide'=16,'shard'=2] {'wide','shard'}, use_global_device_ids=true, to_apply=%region_3.5 | all-reduce | flops 2 | bytes 16 | tf_op jit(solution)/shard_map/psum | solution.py:66
  165.8 22.8 %all_gather.7 = bf16[1,64,32,128]{3,2,0,1:T(8,128)(2,1)S(1)} all-gather(bf16[1,4,32,128]{3,2,0,1:T(8,128)(2,1)S(1)} %divide_convert_fusion), channel_id=1, replica_groups=mesh['wide'=16,'shard'=2] {'wide'}, dimensions={1}, use_global_device_ids=true | all-gather | bytes 557056 | tf_op jit(solution)/shard_map/all_gather | solution.py:69
  188.8 18.9 %all_gather.6 = bf16[1,64,32,128]{3,2,0,1:T(8,128)(2,1)S(1)} all-gather(bf16[1,4,32,128]{3,2,0,1:T(8,128)(2,1)S(1)} %divide_convert_fusion.1), channel_id=1, replica_groups=mesh['wide'=16,'shard'=2] {'wide'}, dimensions={1}, use_global_device_ids=true | all-gather | bytes 557056 | tf_op jit(solution)/shard_map/all_gather | solution.py:69
  210.0 2.4 %fusion.8 = f32[64,32,128]{2,1,0:T(8,128)S(1)} fusion(f32[64,32,128]{2,1,0:T(8,128)} %gather_fusion.4, pred[64]{0:T(512)(128)(4,1)S(1)} %and_bitcast_fusion, f32[128]{0:T(128)S(1)} %get-tuple-element.41, f32[128]{0:T(128)S(1)} %get-tuple-element.42), kind=kOutput, calls=%fused_computation.23 | convolution fusion | flops 402964480 | bytes 2098240 | tf_op jit(solution)/shard_map/rjpc,cb->rjpb/dot_general | solution.py:30
  213.7 6.7 %fusion.60 = f32[64,128,128]{2,1,0:T(8,128)S(1)} fusion(f32[64,32,128]{2,1,0:T(8,128)S(1)} %fusion.11, f32[64,32,128]{2,1,0:T(8,128)S(1)} %bitcast.201), kind=kOutput, calls=%fused_computation.104 | convolution fusion | flops 402653184 | bytes 6291456 | tf_op jit(solution)/shard_map/rjpa,rjpb->rajb/dot_general | solution.py:31
  220.4 7.4 %fusion.1 = bf16[1,128,64,128]{1,3,2,0:T(8,128)(2,1)S(1)} fusion(f32[1,128,64,128]{1,3,2,0:T(8,128)S(1)} %bitcast.203, f32[64,128,128]{2,1,0:T(8,128)S(1)} %fusion.60, f32[64,32,128]{2,1,0:T(8,128)S(1)} %fusion.8, f32[64,32,128]{2,1,0:T(8,128)S(1)} %bitcast.202), kind=kOutput, calls=%fused_computation.8 | convolution fusion | flops 407896064 | bytes 12582912 | tf_op jit(solution)/shard_map/rjpa,rjpb->rajb/dot_general | solution.py:31
  227.8 2.9 %copy.50 = bf16[128,8192]{1,0:T(8,128)(2,1)} copy(bf16[128,8192]{0,1:T(8,128)(2,1)S(1)} %bitcast.209) | data formatting | bytes 4194304
  (54 shorter events, 20.3 us)
Async XLA Ops:
  10.0 2.7 %copy-start.2 = (bf16[1,128,8192]{2,1,0:T(8,128)(2,1)S(1)}, bf16[1,128,8192]{2,1,0:T(8,128)(2,1)}, u32[]{:S(2)}) copy-start(bf16[1,128,8192]{2,1,0:T(8,128)(2,1)} %param.10) | copy-start | bytes 6291460
  66.2 7.9 %copy-start = (f32[1,128,64,128]{1,3,2,0:T(8,128)}, f32[1,128,64,128]{1,3,2,0:T(8,128)S(1)}, u32[]{:S(2)}) copy-start(f32[1,128,64,128]{1,3,2,0:T(8,128)S(1)} %fusion.3) | copy-start | bytes 12582916
  78.5 21.7 %all-to-all-start.1 = ((bf16[1,64,32,128]{3,2,0,1:T(8,128)(2,1)}), bf16[1,64,32,128]{3,2,0,1:T(8,128)(2,1)S(1)}, u32[]{:S(2)}, u32[]{:S(2)}) async-start(bf16[1,64,32,128]{3,2,0,1:T(8,128)(2,1)} %get-tuple-element.39), calls=%async_computation.1 | async-start | bytes 1048576 | tf_op jit(solution)/shard_map/all_to_all | solution.py:58
  100.2 0.8 copy-start.3
  101.0 20.5 %all-to-all-start = ((bf16[1,64,32,128]{3,2,0,1:T(8,128)(2,1)}), bf16[1,64,32,128]{3,2,0,1:T(8,128)(2,1)}, u32[]{:S(2)}, u32[]{:S(2)}) async-start(bf16[1,64,32,128]{3,2,0,1:T(8,128)(2,1)} %get-tuple-element.40), calls=%async_computation | async-start | bytes 1048576 | tf_op jit(solution)/shard_map/all_to_all | solution.py:58
  117.0 4.4 %copy-start.9 = (s32[1,64]{1,0:T(1,128)S(1)}, s32[1,64]{1,0:T(1,128)}, u32[]{:S(2)}) copy-start(s32[1,64]{1,0:T(1,128)} %param.13) | copy-start | bytes 772
  117.0 4.4 %copy-start.4 = (bf16[1,64,32,128]{3,2,0,1:T(8,128)(2,1)S(1)}, bf16[1,64,32,128]{3,2,0,1:T(8,128)(2,1)}, u32[]{:S(2)}) copy-start(bf16[1,64,32,128]{3,2,0,1:T(8,128)(2,1)} %copy-done.3) | copy-start | bytes 1572868
  117.0 5.6 %copy-start.5 = (f32[1,4,32,128]{3,2,1,0:T(8,128)S(1)}, f32[1,4,32,128]{3,2,1,0:T(8,128)}, u32[]{:S(2)}) copy-start(f32[1,4,32,128]{3,2,1,0:T(8,128)} %param.15) | copy-start | bytes 196612
  117.0 5.6 %copy-start.6 = (f32[1,4,32,128]{3,2,1,0:T(8,128)S(1)}, f32[1,4,32,128]{3,2,1,0:T(8,128)}, u32[]{:S(2)}) copy-start(f32[1,4,32,128]{3,2,1,0:T(8,128)} %param.14) | copy-start | bytes 196612
  123.4 86.6 %copy-start.7 = (f32[1,4,32,128]{3,2,0,1:T(8,128)}, f32[1,4,32,128]{3,2,0,1:T(8,128)S(1)}, u32[]{:S(2)}) copy-start(f32[1,4,32,128]{3,2,0,1:T(8,128)S(1)} %get-tuple-element.31) | copy-start | bytes 196612
  123.4 86.6 %copy-start.8 = (f32[1,4,32,128]{3,2,0,1:T(8,128)}, f32[1,4,32,128]{3,2,0,1:T(8,128)S(1)}, u32[]{:S(2)}) copy-start(f32[1,4,32,128]{3,2,0,1:T(8,128)S(1)} %get-tuple-element.32) | copy-start | bytes 196612
  212.5 8.0 %copy-start.1 = (f32[128,8192]{0,1:T(8,128)S(1)}, f32[128,8192]{0,1:T(8,128)}, u32[]{:S(2)}) copy-start(f32[128,8192]{0,1:T(8,128)} %copy.35) | copy-start | bytes 12582916
where the time goes:
time: 236 us; the launch traced here: 232 us
  blocking collectives  82.6 us (35%)
  matrix products  61.7 us (26%)
  local copies, waits for them, and re-layouts  44.2 us (19%)
  other arithmetic  16.5 us (7%)
  waiting for transfers between devices  12.1 us (5%)
  starting transfers between devices  11.9 us (5%)
  between operations  2.56 us (1%)
    all_gather x2, blocking collectives, per_device(): gathered = lax.all_gather(update, 'wide', axis=1, tiled=True)  41.7 us
    psum x1, blocking collectives, per_device(): power_sum = lax.psum(jnp.sum(raw_update * raw_update), ('wide', 'shard'))  40.9 us
    dot_general x4, matrix products, inverse(): return jnp.einsum('rjpa,rjpb->rajb', picked, right_part, precision=highest)  32.9 us
    dot_general x2, matrix products, per_device(): jnp.einsum('rjpa,rajb->rjpb', picked, blended, precision=highest)  19.4 us
    unnamed x25, local copies, waits for them, and re-layouts  12.7 us
    all_to_all x2, waiting for transfers between devices, per_device(): lax.all_to_all(slot_band.astype(jnp.bfloat16), 'wide', split_axis=1, conc...  12.1 us
    all_to_all x2, starting transfers between devices, per_device(): lax.all_to_all(slot_band.astype(jnp.bfloat16), 'wide', split_axis=1, conc...  11.9 us
    convert_element_type x2, local copies, waits for them, and re-layouts, per_device(): grads[step_index, 0].astype(jnp.float32).reshape(block_shape)  11.2 us
  transfers between devices with their start and end apart: 2, of which 1 were waited for; matrix products, arithmetic and copies ran while one was open for 8% of the time, Pallas kernels for 0%

commit v1 on v0

--- a/solution.py
+++ b/solution.py
@@ -11,6 +11,12 @@
 adam_eps = 1e-08
 rms_eps = 1e-06
 learning_rate = 0.2
+
+
+def swap_blocks(x, axis, split, join):
+    shards = jnp.split(x, lax.axis_size(axis), axis=split)
+    got = lax.all_to_all(jnp.stack(shards), axis, 0, 0)
+    return jnp.concatenate(got, axis=join)
 
 
 def dct_table(length):
@@ -55,9 +61,7 @@
         band_coef = jnp.einsum("rjpb,cb->rjpc", left_part, basis, precision=highest)
         moment_now = blended - inverse(band_coef, picked, basis)
         slot_band = jnp.take_along_axis(band_coef, slot_order[:, :, None, None], axis=1)
-        pieces = lax.all_to_all(
-            slot_band.astype(jnp.bfloat16), "wide", split_axis=1, concat_axis=0, tiled=True
-        ).astype(slot_band.dtype)
+        pieces = swap_blocks(slot_band.astype(jnp.bfloat16), "wide", 1, 0).astype(slot_band.dtype)
         summed = jnp.sum(pieces.reshape((replicas, row_blocks) + pieces.shape[1:]), axis=0)
         mean_band = summed / replicas
         avg_now = beta_one * avg_now + (1.0 - beta_one) * mean_band

time: 236 us -> 244 us (1.034)
  local copies, waits for them, and re-layouts: 44.2 us -> 63.8 us
  waiting for transfers between devices: 12.1 us -> 2.21 us
    unnamed x25 -> x55, local copies, waits for them, and re-layouts: 12.7 us -> 31 us
    all_to_all x2, waiting for transfers between devices: 12.1 us -> 2.21 us  [swap_blocks(): got = lax.all_to_all(jnp.stack(shards), axis, 0, 0)]
  transfers between devices with their start and end apart: 2 -> 2, of which waited for: 1 -> 1; matrix products, arithmetic and copies ran while one was open for 8% -> 12% of each run, Pallas kernels for 0% -> 0%
where the time goes in v1:
time: 244 us; the launch traced here: 240 us
  blocking collectives  82.4 us (34%)
  local copies, waits for them, and re-layouts  63.8 us (26%)
  matrix products  61.7 us (25%)
  other arithmetic  15.5 us (6%)
  starting transfers between devices  11.9 us (5%)
  between operations  2.59 us (1%)
    all_gather x2, blocking collectives, per_device(): gathered = lax.all_gather(update, 'wide', axis=1, tiled=True)  41.7 us
    psum x1, blocking collectives, per_device(): power_sum = lax.psum(jnp.sum(raw_update * raw_update), ('wide', 'shard'))  40.8 us
    dot_general x4, matrix products, inverse(): return jnp.einsum('rjpa,rjpb->rajb', picked, right_part, precision=highest)  32.9 us
    unnamed x55, local copies, waits for them, and re-layouts  31 us
    dot_general x2, matrix products, per_device(): jnp.einsum('rjpa,rajb->rjpb', picked, blended, precision=highest)  19.4 us
    all_to_all x2, starting transfers between devices, swap_blocks(): got = lax.all_to_all(jnp.stack(shards), axis, 0, 0)  11.9 us
    convert_element_type x2, local copies, waits for them, and re-layouts, per_device(): grads[step_index, 0].astype(jnp.float32).reshape(block_shape)  11.2 us
    dot_general x4, matrix products, inverse(): right_part = jnp.einsum('rjpc,cb->rjpb', coefs, basis, precision=highest)  7.04 us
  transfers between devices with their start and end apart: 2, of which 1 were waited for; matrix products, arithmetic and copies ran while one was open for 12% of the time, Pallas kernels for 0%

profile of v1, /device:TPU:0, one launch (start us, length us, event | category | flops | bytes accessed | tf_op | source)
XLA Modules:
  0.0 240.0 jit_solution(2538649339158480120)
XLA Ops:
  3.4 6.6 %slice_convert_fusion.1 = (f32[1,1,128,8192]{3,2,1,0:T(8,128)}, f32[16,8,64,128]{3,1,2,0:T(8,128)S(1)}, f32[1,1,128,8192]{3,2,1,0:T(8,128)}) fusion(bf16[2,1,128,8192]{3,2,1,0:T(8,128)(2,1)} %param.11), kind=kLoop, calls=%fused_computation.20 | loop fusion | flops 2097152 | bytes 16777216 | tf_op jit(solution)/shard_map/convert_element_type | solution.py:57
  10.0 2.7 %copy.54 = f32[16,8,64,128]{3,2,1,0:T(8,128)} copy(f32[16,8,64,128]{3,1,2,0:T(8,128)S(1)} %get-tuple-element.34) | data formatting | bytes 8388608
  12.7 2.5 %convert_multiply_fusion = (f32[1,128,8192]{2,1,0:T(8,128)}, f32[16,8,64,128]{3,1,2,0:T(8,128)S(1)}) fusion(bf16[1,128,8192]{2,1,0:T(8,128)(2,1)S(1)} %copy-done.2), kind=kLoop, calls=%fused_computation.18 | loop fusion | flops 2097152 | bytes 10485760 | tf_op jit(solution)/shard_map/mul | solution.py:57
  15.3 2.7 %copy.53 = f32[16,8,64,128]{3,2,1,0:T(8,128)} copy(f32[16,8,64,128]{3,1,2,0:T(8,128)S(1)} %get-tuple-element.37) | data formatting | bytes 8388608
  18.2 6.0 %gather_fusion = f32[2048,128]{1,0:T(8,128)S(1)} fusion(f32[128,128]{1,0:T(8,128)S(1)} %cosine_multiply_fusion, s32[2048]{0:T(1024)S(1)} %broadcast_clamp_fusion), kind=kCustom, calls=%fused_computation.4 | custom fusion | bytes 2105344 | tf_op jit(solution)/shard_map/gather | solution.py:32
  24.2 12.7 %fusion.6 = f32[64,32,128]{2,1,0:T(8,128)S(1)} fusion(f32[64,32,128]{2,1,0:T(8,128)S(1)} %bitcast.313, f32[128,64,128]{2,1,0:T(8,128)} %bitcast.320, f32[128,64,128]{2,1,0:T(8,128)} %bitcast.321), kind=kOutput, calls=%fused_computation.16 | convolution fusion | flops 403701760 | bytes 10485760 | tf_op jit(solution)/shard_map/rjpa,rajb->rjpb/dot_general | solution.py:60
  39.3 5.6 %copy.43 = f32[1,1,128,8192]{2,3,1,0:T(8,128)} copy(f32[1,1,128,8192]{3,2,1,0:T(8,128)} %get-tuple-element.33) | data formatting | bytes 8388608 | tf_op jit(solution)/shard_map/convert_element_type | solution.py:57
  44.9 5.6 %copy.44 = f32[1,1,128,8192]{2,3,1,0:T(8,128)} copy(f32[1,1,128,8192]{3,2,1,0:T(8,128)} %get-tuple-element.35) | data formatting | bytes 8388608 | tf_op jit(solution)/shard_map/convert_element_type | solution.py:57
  50.5 5.6 %copy.42 = f32[1,128,8192]{1,2,0:T(8,128)} copy(f32[1,128,8192]{2,1,0:T(8,128)} %get-tuple-element.36) | data formatting | bytes 8388608 | tf_op jit(solution)/shard_map/mul | solution.py:57
  56.1 10.1 %fusion.3 = f32[1,128,64,128]{1,3,2,0:T(8,128)S(1)} fusion(f32[1,128,64,128]{1,3,2,0:T(8,128)} %bitcast.323, f32[1,128,64,128]{1,3,2,0:T(8,128)} %bitcast.324, f32[1,128,64,128]{1,3,2,0:T(8,128)} %bitcast.322, f32[64,32,128]{2,1,0:T(8,128)S(1)} %fusion.25, f32[64,32,128]{2,1,0:T(8,128)S(1)} %bitcast.314), kind=kOutput, calls=%fused_computation.11 | convolution fusion | flops 406847488 | bytes 18874368 | tf_op jit(solution)/shard_map/rjpa,rjpb->rajb/dot_general | solution.py:37
  66.2 6.7 %fusion.4 = f32[64,32,128]{2,1,0:T(8,128)S(1)} fusion(f32[64,32,128]{2,1,0:T(8,128)S(1)} %bitcast.315, f32[1,128,64,128]{1,3,2,0:T(8,128)S(1)} %fusion.3), kind=kOutput, calls=%fused_computation.13 | convolution fusion | flops 402653184 | bytes 6291456 | tf_op jit(solution)/shard_map/rjpa,rajb->rjpb/dot_general | solution.py:60
  87.2 7.4 %all-to-all-start = ((bf16[16,1,4,32,128]{4,3,2,1,0:T(8,128)(2,1)}), bf16[16,1,4,32,128]{4,3,2,1,0:T(8,128)(2,1)S(1)}, u32[]{:S(2)}, u32[]{:S(2)}) async-start(bf16[16,1,4,32,128]{4,3,2,1,0:T(8,128)(2,1)} %constant_dynamic-update-slice_fusion), calls=%async_computation | async-start | bytes 1048576 | tf_op jit(solution)/shard_map/all_to_all | solution.py:18
  106.7 2.2 all-to-all-done
  109.7 4.4 %all-to-all-start.1 = ((bf16[16,1,4,32,128]{4,3,2,1,0:T(8,128)(2,1)}), bf16[16,1,4,32,128]{4,3,2,1,0:T(8,128)(2,1)}, u32[]{:S(2)}, u32[]{:S(2)}) async-start(bf16[16,1,4,32,128]{4,3,2,1,0:T(8,128)(2,1)} %constant_dynamic-update-slice_fusion.16), calls=%async_computation.1 | async-start | bytes 1048576 | tf_op jit(solution)/shard_map/all_to_all | solution.py:18
  114.2 8.7 %fusion = bf16[1,128,64,128]{1,3,2,0:T(8,128)(2,1)S(1)} fusion(f32[1,128,64,128]{1,3,2,0:T(8,128)} %copy-done, f32[64,32,128]{2,1,0:T(8,128)} %fusion.20, f32[64,32,128]{2,1,0:T(8,128)S(1)} %bitcast.316), kind=kOutput, calls=%fused_computation.6 | convolution fusion | flops 404750336 | bytes 8388608 | tf_op jit(solution)/shard_map/rjpa,rjpb->rajb/dot_general | solution.py:37
  122.8 2.9 %copy.49 = bf16[1,128,8192]{2,1,0:T(8,128)(2,1)} copy(bf16[1,128,8192]{1,2,0:T(8,128)(2,1)S(1)} %bitcast.326) | data formatting | bytes 4194304
  125.8 4.4 %copy.35 = f32[128,8192]{0,1:T(8,128)} copy(bf16[128,8192]{1,0:T(8,128)(2,1)} %param.9) | data formatting | bytes 6291456 | tf_op jit(solution)/shard_map/reshape | solution.py:51
  132.1 40.8 %all-reduce = (f32[]{:T(128)}, f32[]{:T(128)}) all-reduce(f32[]{:T(128)} %get-tuple-element.38, f32[]{:T(128)} %get-tuple-element.30), channel_id=1, replica_groups=mesh['wide'=16,'shard'=2] {'wide','shard'}, use_global_device_ids=true, to_apply=%region_3.5 | all-reduce | flops 2 | bytes 16 | tf_op jit(solution)/shard_map/psum | solution.py:70
  174.3 22.8 %all_gather.7 = bf16[1,64,32,128]{3,2,0,1:T(8,128)(2,1)S(1)} all-gather(bf16[1,4,32,128]{3,2,0,1:T(8,128)(2,1)S(1)} %divide_convert_fusion), channel_id=1, replica_groups=mesh['wide'=16,'shard'=2] {'wide'}, dimensions={1}, use_global_device_ids=true | all-gather | bytes 557056 | tf_op jit(solution)/shard_map/all_gather | solution.py:73
  197.3 18.9 %all_gather.6 = bf16[1,64,32,128]{3,2,0,1:T(8,128)(2,1)S(1)} all-gather(bf16[1,4,32,128]{3,2,0,1:T(8,128)(2,1)S(1)} %divide_convert_fusion.1), channel_id=1, replica_groups=mesh['wide'=16,'shard'=2] {'wide'}, dimensions={1}, use_global_device_ids=true | all-gather | bytes 557056 | tf_op jit(solution)/shard_map/all_gather | solution.py:73
  218.5 2.4 %fusion.8 = f32[64,32,128]{2,1,0:T(8,128)S(1)} fusion(f32[64,32,128]{2,1,0:T(8,128)} %gather_fusion.4, pred[64]{0:T(512)(128)(4,1)S(1)} %and_bitcast_fusion, f32[128]{0:T(128)S(1)} %get-tuple-element.41, f32[128]{0:T(128)S(1)} %get-tuple-element.42), kind=kOutput, calls=%fused_computation.21 | convolution fusion | flops 402964480 | bytes 2098240 | tf_op jit(solution)/shard_map/rjpc,cb->rjpb/dot_general | solution.py:36
  222.2 6.7 %fusion.58 = f32[64,128,128]{2,1,0:T(8,128)S(1)} fusion(f32[64,32,128]{2,1,0:T(8,128)S(1)} %fusion.11, f32[64,32,128]{2,1,0:T(8,128)S(1)} %bitcast.317), kind=kOutput, calls=%fused_computation.166 | convolution fusion | flops 402653184 | bytes 6291456 | tf_op jit(solution)/shard_map/rjpa,rjpb->rajb/dot_general | solution.py:37
  228.9 7.4 %fusion.1 = bf16[1,128,64,128]{1,3,2,0:T(8,128)(2,1)S(1)} fusion(f32[1,128,64,128]{1,3,2,0:T(8,128)S(1)} %bitcast.319, f32[64,128,128]{2,1,0:T(8,128)S(1)} %fusion.58, f32[64,32,128]{2,1,0:T(8,128)S(1)} %fusion.8, f32[64,32,128]{2,1,0:T(8,128)S(1)} %bitcast.318), kind=kOutput, calls=%fused_computation.8 | convolution fusion | flops 407896064 | bytes 12582912 | tf_op jit(solution)/shard_map/rjpa,rjpb->rajb/dot_general | solution.py:37
  236.3 2.9 %copy.48 = bf16[128,8192]{1,0:T(8,128)(2,1)} copy(bf16[128,8192]{0,1:T(8,128)(2,1)S(1)} %bitcast.325) | data formatting | bytes 4194304
  (86 shorter events, 38.9 us)
Async XLA Ops:
  10.0 2.7 %copy-start.2 = (bf16[1,128,8192]{2,1,0:T(8,128)(2,1)S(1)}, bf16[1,128,8192]{2,1,0:T(8,128)(2,1)}, u32[]{:S(2)}) copy-start(bf16[1,128,8192]{2,1,0:T(8,128)(2,1)} %param.10) | copy-start | bytes 6291460
  66.2 7.9 %copy-start = (f32[1,128,64,128]{1,3,2,0:T(8,128)}, f32[1,128,64,128]{1,3,2,0:T(8,128)S(1)}, u32[]{:S(2)}) copy-start(f32[1,128,64,128]{1,3,2,0:T(8,128)S(1)} %fusion.3) | copy-start | bytes 12582916
  87.2 21.7 %all-to-all-start = ((bf16[16,1,4,32,128]{4,3,2,1,0:T(8,128)(2,1)}), bf16[16,1,4,32,128]{4,3,2,1,0:T(8,128)(2,1)S(1)}, u32[]{:S(2)}, u32[]{:S(2)}) async-start(bf16[16,1,4,32,128]{4,3,2,1,0:T(8,128)(2,1)} %constant_dynamic-update-slice_fusion), calls=%async_computation | async-start | bytes 1048576 | tf_op jit(solution)/shard_map/all_to_all | solution.py:18
  108.9 0.8 copy-start.3
  109.7 20.5 %all-to-all-start.1 = ((bf16[16,1,4,32,128]{4,3,2,1,0:T(8,128)(2,1)}), bf16[16,1,4,32,128]{4,3,2,1,0:T(8,128)(2,1)}, u32[]{:S(2)}, u32[]{:S(2)}) async-start(bf16[16,1,4,32,128]{4,3,2,1,0:T(8,128)(2,1)} %constant_dynamic-update-slice_fusion.16), calls=%async_computation.1 | async-start | bytes 1048576 | tf_op jit(solution)/shard_map/all_to_all | solution.py:18
  125.7 4.4 %copy-start.9 = (s32[1,64]{1,0:T(1,128)S(1)}, s32[1,64]{1,0:T(1,128)}, u32[]{:S(2)}) copy-start(s32[1,64]{1,0:T(1,128)} %param.13) | copy-start | bytes 772
  125.7 4.4 %copy-start.4 = (bf16[16,1,4,32,128]{4,3,2,1,0:T(8,128)(2,1)S(1)}, bf16[16,1,4,32,128]{4,3,2,1,0:T(8,128)(2,1)}, u32[]{:S(2)}) copy-start(bf16[16,1,4,32,128]{4,3,2,1,0:T(8,128)(2,1)} %copy-done.3) | copy-start | bytes 1572868
  125.7 5.6 %copy-start.5 = (f32[1,4,32,128]{3,2,1,0:T(8,128)S(1)}, f32[1,4,32,128]{3,2,1,0:T(8,128)}, u32[]{:S(2)}) copy-start(f32[1,4,32,128]{3,2,1,0:T(8,128)} %param.15) | copy-start | bytes 196612
  125.7 5.6 %copy-start.6 = (f32[1,4,32,128]{3,2,1,0:T(8,128)S(1)}, f32[1,4,32,128]{3,2,1,0:T(8,128)}, u32[]{:S(2)}) copy-start(f32[1,4,32,128]{3,2,1,0:T(8,128)} %param.14) | copy-start | bytes 196612
  132.1 86.4 %copy-start.7 = (f32[1,4,32,128]{3,2,0,1:T(8,128)}, f32[1,4,32,128]{3,2,0,1:T(8,128)S(1)}, u32[]{:S(2)}) copy-start(f32[1,4,32,128]{3,2,0,1:T(8,128)S(1)} %get-tuple-element.31) | copy-start | bytes 196612
  132.1 86.4 %copy-start.8 = (f32[1,4,32,128]{3,2,0,1:T(8,128)}, f32[1,4,32,128]{3,2,0,1:T(8,128)S(1)}, u32[]{:S(2)}) copy-start(f32[1,4,32,128]{3,2,0,1:T(8,128)S(1)} %get-tuple-element.32) | copy-start | bytes 196612
  221.0 7.9 %copy-start.1 = (f32[128,8192]{0,1:T(8,128)S(1)}, f32[128,8192]{0,1:T(8,128)}, u32[]{:S(2)}) copy-start(f32[128,8192]{0,1:T(8,128)} %copy.35) | copy-start | bytes 12582916
